TPU v7x, 512 devices: a whole 4x8x8 slice. The times are simulated.
512 devices in a mesh: row: 32 (over z, y_lo), col: 16 (over y_hi, x, core).
Axes of the slice: x: 4, y: 8 (y_hi: 2, y_lo: 4; y = y_hi * 4 + y_lo), z: 8, core: 2. Of those that a mesh axis runs over, the one named last changes fastest.
Arguments:
- features: bfloat16 [16, 4096, 128], P('col', 'row'), may hold values from -6 to 6
- weight1: bfloat16 [128, 128], replicated, may hold values from -0.5 to 0.5
- weight2: bfloat16 [128, 128], replicated, may hold values from -0.5 to 0.5
- tile_values: bfloat16 [32, 16, 96, 128, 128], P('row', 'col'), may hold values from -0.1875 to 0.1875
- tile_coords: int32 [32, 16, 2, 96], P('row', 'col'), may hold values from 0 to 31, as said below
- tile_count: int32 [32, 16], P('row', 'col'), may hold values from 1 to 96, as said below
- out_grad: bfloat16 [16, 4096, 128], P('col', 'row'), may hold values from -6 to 6
Outputs:
- output: bfloat16 [16, 4096, 128], P('col', 'row')
- grad_features: bfloat16 [16, 4096, 128], P('col', 'row')
- grad_weight1: float32 [128, 128], replicated
- grad_weight2: float32 [128, 128], replicated
Inputs may be any that keep to these rules, and one draw needn't show every extreme that they name: On each device tile_coords[r, c, 0, t] is below 16 and tile_coords[r, c, 1, t] below 32; no block position appears twice among a device's 96 slots. `tile_count`: some device has all 96 slots live.
All inputs are finite; a program needn't handle non-finite values.
Results may differ from a plain program's by a relative error of at most 0.034.
Values may be sent and summed in bfloat16 or wider, within the bound.
No kernel may reach another device: no remote copies, remote signals or barrier semaphores. Data moves between devices by JAX's collectives and lax.ppermute only.
A program may use at most 64 MiB of HBM per device.

v0:
```python
import math
import jax
import jax.numpy as jnp
from jax import lax
from jax.sharding import PartitionSpec as P


def forward_part(local_tiles, row_ids, col_ids, live_slots, panel_rows, row_blocks):
    block_side = local_tiles.shape[1]
    feat_width = panel_rows.shape[-1]
    blocks = panel_rows.reshape(-1, block_side, feat_width)[col_ids]
    products = jnp.einsum("tij,tjf->tif", local_tiles, blocks, preferred_element_type=jnp.float32)
    onehot = jnp.where(
        (row_ids[None, :] == jnp.arange(row_blocks, dtype=jnp.int32)[:, None])
        & live_slots[None, :],
        1.0,
        0.0,
    ).astype(jnp.float32)
    return jnp.einsum("rt,tif->rif", onehot, products).reshape(row_blocks * block_side, feat_width)


def transposed_part(local_tiles, row_ids, col_ids, live_slots, panel_rows, col_blocks):
    block_side = local_tiles.shape[1]
    feat_width = panel_rows.shape[-1]
    blocks = panel_rows.reshape(-1, block_side, feat_width)[row_ids]
    products = jnp.einsum("tji,tjf->tif", local_tiles, blocks, preferred_element_type=jnp.float32)
    onehot = jnp.where(
        (col_ids[None, :] == jnp.arange(col_blocks, dtype=jnp.int32)[:, None])
        & live_slots[None, :],
        1.0,
        0.0,
    ).astype(jnp.float32)
    return jnp.einsum("ct,tif->cif", onehot, products).reshape(col_blocks * block_side, feat_width)


def silu_slope(value):
    sigmoid = jax.nn.sigmoid(value)
    return sigmoid * (1.0 + value * (1.0 - sigmoid))


def on_device(features, weight1, weight2, tile_values, tile_coords, tile_count, out_grad):
    local_tiles = tile_values[0, 0]
    row_ids = tile_coords[0, 0, 0]
    col_ids = tile_coords[0, 0, 1]
    slot_total = local_tiles.shape[0]
    live_slots = jnp.arange(slot_total, dtype=jnp.int32) < tile_count[0, 0]
    block_side = local_tiles.shape[1]
    shard_rows = features.shape[1]
    row_blocks = shard_rows * lax.axis_size("col") // block_side
    col_blocks = shard_rows * lax.axis_size("row") // block_side
    node_total = shard_rows * lax.axis_size("row") * lax.axis_size("col")
    grad_local = out_grad[0]
    grad_two = jnp.dot(grad_local, weight2.T, preferred_element_type=jnp.float32).astype(
        jnp.bfloat16
    )
    gathered = lax.all_gather(features, "row", axis=1, tiled=True)[0]
    grad_rows = lax.all_gather(grad_two, "row", axis=0, tiled=True)
    part_one = forward_part(local_tiles, row_ids, col_ids, live_slots, gathered, row_blocks)
    part_three = forward_part(local_tiles, row_ids, col_ids, live_slots, grad_rows, row_blocks)
    agg_sum, grad_hidden = (
        lax.psum_scatter(
            part_one.astype(jnp.bfloat16), "col", scatter_dimension=0, tiled=True
        ).astype(jnp.float32),
        lax.psum_scatter(
            part_three.astype(jnp.bfloat16), "col", scatter_dimension=0, tiled=True
        ).astype(jnp.float32),
    )
    agg_one = agg_sum.astype(jnp.bfloat16)
    pre_one = jnp.dot(agg_one, weight1, preferred_element_type=jnp.float32)
    hidden = jax.nn.silu(pre_one).astype(jnp.bfloat16)
    hidden_rows = lax.all_gather(hidden, "col", axis=0, tiled=True)
    part_two = transposed_part(local_tiles, row_ids, col_ids, live_slots, hidden_rows, col_blocks)
    agg_two = lax.psum_scatter(
        part_two.astype(jnp.bfloat16), "row", scatter_dimension=0, tiled=True
    )
    output = jnp.dot(agg_two, weight2, preferred_element_type=jnp.float32).astype(jnp.bfloat16)
    grad_pre = (grad_hidden * silu_slope(pre_one)).astype(jnp.bfloat16)
    grad_one = jnp.dot(grad_pre, weight1.T, preferred_element_type=jnp.float32).astype(jnp.bfloat16)
    grad_hidden_rows = lax.all_gather(grad_one, "col", axis=0, tiled=True)
    part_four = transposed_part(
        local_tiles, row_ids, col_ids, live_slots, grad_hidden_rows, col_blocks
    )
    grad_features = lax.psum_scatter(
        part_four.astype(jnp.bfloat16), "row", scatter_dimension=0, tiled=True
    )
    contract = (((0,), (0,)), ((), ()))
    weight_one = lax.dot_general(agg_one, grad_pre, contract, preferred_element_type=jnp.float32)
    weight_two = lax.dot_general(agg_two, grad_local, contract, preferred_element_type=jnp.float32)
    sum_one, sum_two = lax.psum((weight_one, weight_two), ("row", "col"))
    factor = 1.0 / math.sqrt(node_total)
    return (output[None], grad_features[None], sum_one * factor, sum_two * factor)


def solution(mesh):
    placed = (
        P("col", "row", None),
        P(),
        P(),
        P("row", "col", None, None, None),
        P("row", "col", None, None),
        P("row", "col"),
        P("col", "row", None),
    )
    return jax.shard_map(
        on_device,
        mesh=mesh,
        in_specs=placed,
        out_specs=(P("col", "row", None), P("col", "row", None), P(), P()),
        check_vma=False,
    )
```

profile of v0, /device:TPU:2, one launch (start us, length us, event | category | flops | bytes accessed | tf_op | source)
XLA Modules:
  0.0 1141.4 jit_solution(11435500891429155768)
XLA Ops:
  7.2 0.0 all-gather.5.cloned.1.call-start
  7.2 1.7 convolution_convert_fusion.1
  8.9 0.0 all-gather.5.cloned.1.call-update
  8.9 0.0 all-gather.3.cloned.1.call-start
  9.0 0.7 all-gather.3.cloned.1.call-update
  9.7 0.0 reduce-scatter.9.cloned.1.call-start
  10.4 0.8 fusion.63
  11.2 0.8 slice_bitcast_fusion.1
  11.9 156.6 %all-gather.5.cloned.1.call-done = bf16[4096,128]{1,0:T(8,128)(2,1)} async-done(((bf16[128,128]{1,0:T(8,128)(2,1)}), bf16[4096,128]{1,0:T(8,128)(2,1)}) %all-gather.5.cloned.1.call-update) | async-done | bytes 1048592 | tf_op jit(solution)/shard_map/all_gather | solution.py:57
  168.5 3.9 gather_fusion.2
  172.5 5.9 fusion.10
  178.4 5.0 copy.18
  183.3 2.4 fusion.25
  185.8 1.0 copy.14
  186.7 0.0 reduce-scatter.9.cloned.1.call-update
  186.7 0.0 reduce-scatter.5.cloned.1.call-start
  186.8 137.2 %all-gather.3.cloned.1.call-done = bf16[1,4096,128]{2,1,0:T(8,128)(2,1)} async-done(((bf16[1,128,128]{2,1,0:T(8,128)(2,1)}), bf16[1,4096,128]{2,1,0:T(8,128)(2,1)}) %all-gather.3.cloned.1.call-update) | async-done | bytes 1048592 | tf_op jit(solution)/shard_map/all_gather | solution.py:56
  324.0 3.9 gather_fusion
  327.9 5.9 fusion.14
  333.9 5.0 copy.16
  338.8 2.4 fusion.22
  341.2 1.0 copy.12
  342.2 0.0 reduce-scatter.7.cloned.1.call-start
  342.3 71.1 %reduce-scatter.9.cloned.1.call-done = bf16[128,128]{1,0:T(8,128)(2,1)} async-done(((bf16[2048,128]{1,0:T(8,128)(2,1)}), bf16[128,128]{1,0:T(8,128)(2,1)}) %reduce-scatter.9.cloned.1.call-update) | async-done | bytes 32784 | tf_op jit(solution)/shard_map/reduce_scatter | solution.py:64
  413.4 86.4 %reduce-scatter.5.cloned.1.call-done = bf16[128,128]{1,0:T(8,128)(2,1)} async-done(((bf16[2048,128]{1,0:T(8,128)(2,1)}), bf16[128,128]{1,0:T(8,128)(2,1)}) %reduce-scatter.5.cloned.1.call-update) | async-done | bytes 32784 | tf_op jit(solution)/shard_map/reduce_scatter | solution.py:61
  499.8 0.9 multiply_convert_fusion
  500.8 27.9 %all_gather.13 = bf16[2048,128]{1,0:T(8,128)(2,1)} all-gather(bf16[128,128]{1,0:T(8,128)(2,1)S(1)} %get-tuple-element.7), channel_id=1, replica_groups=mesh['row'=32,'col'=16] {'col'}, dimensions={0}, use_global_device_ids=true | all-gather | bytes 557056 | tf_op jit(solution)/shard_map/all_gather | solution.py:71
  528.7 3.7 gather_fusion.1
  532.4 4.8 fusion.12
  537.2 5.0 copy.17
  542.2 2.4 fusion.16
  544.6 1.4 copy.13
  546.0 0.0 all-reduce.3.cloned.1.call-start
  546.1 0.1 convolution_convert_fusion
  546.2 29.6 %all_gather.15 = bf16[2048,128]{1,0:T(8,128)(2,1)} all-gather(bf16[128,128]{1,0:T(8,128)(2,1)S(1)} %convolution_convert_fusion), channel_id=1, replica_groups=mesh['row'=32,'col'=16] {'col'}, dimensions={0}, use_global_device_ids=true | all-gather | bytes 557056 | tf_op jit(solution)/shard_map/all_gather | solution.py:79
  575.8 3.7 gather_fusion.3
  579.6 4.8 fusion.8
  584.4 5.0 copy.19
  589.3 0.8 fusion.72
  590.2 120.2 %reduce-scatter.7.cloned.1.call-done = bf16[128,128]{1,0:T(8,128)(2,1)} async-done(((bf16[4096,128]{1,0:T(8,128)(2,1)}), bf16[128,128]{1,0:T(8,128)(2,1)}) %reduce-scatter.7.cloned.1.call-update) | async-done | bytes 32784 | tf_op jit(solution)/shard_map/reduce_scatter | solution.py:73
  710.4 1.6 fusion.29
  712.0 0.0 reduce-scatter.11.cloned.1.call-start
  712.0 2.4 fusion.19
  714.5 1.4 copy.15
  715.9 0.8 fusion.28
  716.7 255.6 %all-reduce.3.cloned.1.call-done = (f32[128,128]{1,0:T(8,128)}, f32[128,128]{1,0:T(8,128)}) async-done(((f32[128,128]{1,0:T(8,128)}, f32[128,128]{1,0:T(8,128)}), (f32[128,128]{1,0:T(8,128)}, f32[128,128]{1,0:T(8,128)})) %all-reduce.3.cloned.1.call-update) | async-done | bytes 131088 | tf_op jit(solution)/shard_map/psum | solution.py:89
  972.2 1.5 broadcast_multiply_fusion
  973.8 160.8 %reduce-scatter.11.cloned.1.call-done = bf16[128,128]{1,0:T(8,128)(2,1)} async-done(((bf16[4096,128]{1,0:T(8,128)(2,1)}), bf16[128,128]{1,0:T(8,128)(2,1)}) %reduce-scatter.11.cloned.1.call-update) | async-done | bytes 32784 | tf_op jit(solution)/shard_map/reduce_scatter | solution.py:83
  (19 shorter events, 0.1 us)
Async XLA Ops:
  7.2 165.3 %copy-start = (bf16[1,1,96,128,128]{4,3,2,1,0:T(8,128)(2,1)S(1)}, bf16[1,1,96,128,128]{4,3,2,1,0:T(8,128)(2,1)}, u32[]{:S(2)}) copy-start(bf16[1,1,96,128,128]{4,3,2,1,0:T(8,128)(2,1)} %param.10) | copy-start | bytes 9437188
  7.2 161.4 %all-gather.5.cloned.1.call-start = ((), (), s32[]{:S(2)}) async-start(), calls=%async_computation.7 | async-start | bytes 1081344 | tf_op jit(solution)/shard_map/all_gather | solution.py:57
  8.9 315.1 %all-gather.3.cloned.1.call-start = ((), (), s32[]{:S(2)}) async-start(), calls=%async_computation.4 | async-start | bytes 1081344 | tf_op jit(solution)/shard_map/all_gather | solution.py:56
  9.7 403.7 %reduce-scatter.9.cloned.1.call-start = ((), (), s32[]{:S(2)}) async-start(), calls=%async_computation.8 | async-start | bytes 557056 | tf_op jit(solution)/shard_map/reduce_scatter | solution.py:64
  186.7 313.1 %reduce-scatter.5.cloned.1.call-start = ((), (), s32[]{:S(2)}) async-start(), calls=%async_computation.5 | async-start | bytes 557056 | tf_op jit(solution)/shard_map/reduce_scatter | solution.py:61
  338.8 161.0 %copy-start.4 = (bf16[128,128]{1,0:T(8,128)(2,1)S(1)}, bf16[128,128]{1,0:T(8,128)(2,1)}, u32[]{:S(2)}) copy-start(bf16[128,128]{1,0:T(8,128)(2,1)} %param.8) | copy-start | bytes 98308
  342.2 368.2 %reduce-scatter.7.cloned.1.call-start = ((), (), s32[]{:S(2)}) async-start(), calls=%async_computation.6 | async-start | bytes 1081344 | tf_op jit(solution)/shard_map/reduce_scatter | solution.py:73
  546.0 426.2 %all-reduce.3.cloned.1.call-start = ((), (), s32[]{:S(2)}) async-start(), calls=%async_computation.10 | async-start | bytes 262144 | tf_op jit(solution)/shard_map/psum | solution.py:89
  584.4 5.0 copy-start.5
  584.4 126.0 %copy-start.2 = (bf16[1,128,128]{2,1,0:T(8,128)(2,1)S(1)}, bf16[1,128,128]{2,1,0:T(8,128)(2,1)}, u32[]{:S(2)}) copy-start(bf16[1,128,128]{2,1,0:T(8,128)(2,1)} %param.13) | copy-start | bytes 98308
  712.0 3.9 copy-start.1
  712.0 3.9 copy-start.3
  712.0 422.6 %reduce-scatter.11.cloned.1.call-start = ((), (), s32[]{:S(2)}) async-start(), calls=%async_computation.9 | async-start | bytes 1081344 | tf_op jit(solution)/shard_map/reduce_scatter | solution.py:83
Sparse Core Ops, SparseCore 0:
  10.7 157.8 all-gather.4
  170.6 153.3 all-gather.2
  328.7 84.6 reduce-scatter.8
  418.5 81.2 reduce-scatter.4
  546.1 164.1 reduce-scatter.6
  716.9 255.3 all-reduce.2
  975.6 158.9 reduce-scatter.10
where the time goes:
time: 1140 us
  waiting for transfers between devices  989 us (87%)
  blocking collectives  57.6 us (5%)
  local copies, waits for them, and re-layouts  40.6 us (4%)
  matrix products  37 us (3%)
  between operations  14.9 us (1%)
    psum x1, waiting for transfers between devices, on_device(): sum_one, sum_two = lax.psum((weight_one, weight_two), ('row', 'col'))  256 us
    reduce_scatter x1, waiting for transfers between devices, on_device(): lax.psum_scatter(part_four.astype(jnp.bfloat16), 'row', scatter_dimension...  161 us
    all_gather x1, waiting for transfers between devices, on_device(): grad_rows = lax.all_gather(grad_two, 'row', axis=0, tiled=True)  157 us
    all_gather x1, waiting for transfers between devices, on_device(): gathered = lax.all_gather(features, 'row', axis=1, tiled=True)[0]  137 us
    reduce_scatter x1, waiting for transfers between devices, on_device(): lax.psum_scatter(part_two.astype(jnp.bfloat16), 'row', scatter_dimension=...  120 us
    reduce_scatter x1, waiting for transfers between devices, on_device(): lax.psum_scatter(part_one.astype(jnp.bfloat16), 'col', scatter_dimension=...  86.4 us
    reduce_scatter x1, waiting for transfers between devices, on_device(): lax.psum_scatter(part_three.astype(jnp.bfloat16), 'col', scatter_dimensio...  71.1 us
    all_gather x1, blocking collectives, on_device(): grad_hidden_rows = lax.all_gather(grad_one, 'col', axis=0, tiled=True)  29.6 us
  transfers between devices with their start and end apart: 7, of which 7 were waited for; matrix products, arithmetic and copies ran while one was open for 5% of the time, Pallas kernels for 0%

commit v1 on v0

--- a/solution.py
+++ b/solution.py
@@ -3,6 +3,10 @@
 import jax.numpy as jnp
 from jax import lax
 from jax.sharding import PartitionSpec as P
+
+state_teams_over_axis = lambda packet, ax_name, mesh_ax: lax.psum(
+    lax.psum(packet, axis_name=ax_name), axis_name=mesh_ax
+)
 
 
 def forward_part(local_tiles, row_ids, col_ids, live_slots, panel_rows, row_blocks):
@@ -86,7 +90,7 @@
     contract = (((0,), (0,)), ((), ()))
     weight_one = lax.dot_general(agg_one, grad_pre, contract, preferred_element_type=jnp.float32)
     weight_two = lax.dot_general(agg_two, grad_local, contract, preferred_element_type=jnp.float32)
-    sum_one, sum_two = lax.psum((weight_one, weight_two), ("row", "col"))
+    sum_one, sum_two = state_teams_over_axis((weight_one, weight_two), "col", "row")
     factor = 1.0 / math.sqrt(node_total)
     return (output[None], grad_features[None], sum_one * factor, sum_two * factor)
 

time: 1140 us -> 1350 us (1.18)
  the two profiles are of different devices: /device:TPU:2 before, /device:TPU:4 now
where the time goes in v1:
time: 1350 us
  waiting for transfers between devices  1200 us (89%)
  blocking collectives  55.4 us (4%)
  local copies, waits for them, and re-layouts  40.5 us (3%)
  matrix products  37 us (3%)
  between operations  14.9 us (1%)
    psum x1, waiting for transfers between devices, lax.psum(lax.psum(packet, axis_name=ax_name), axis_name=mesh_ax)  291 us
    reduce_scatter x1, waiting for transfers between devices, on_device(): lax.psum_scatter(part_four.astype(jnp.bfloat16), 'row', scatter_dimension...  163 us
    psum x1, waiting for transfers between devices, lax.psum(packet, axis_name=ax_name)  159 us
    all_gather x1, waiting for transfers between devices, on_device(): grad_rows = lax.all_gather(grad_two, 'row', axis=0, tiled=True)  157 us
    all_gather x1, waiting for transfers between devices, on_device(): gathered = lax.all_gather(features, 'row', axis=1, tiled=True)[0]  137 us
    reduce_scatter x1, waiting for transfers between devices, on_device(): lax.psum_scatter(part_two.astype(jnp.bfloat16), 'row', scatter_dimension=...  133 us
    reduce_scatter x1, waiting for transfers between devices, on_device(): lax.psum_scatter(part_one.astype(jnp.bfloat16), 'col', scatter_dimension=...  86.5 us
    reduce_scatter x1, waiting for transfers between devices, on_device(): lax.psum_scatter(part_three.astype(jnp.bfloat16), 'col', scatter_dimensio...  69.6 us
  transfers between devices with their start and end apart: 8, of which 8 were waited for; matrix products, arithmetic and copies ran while one was open for 4% of the time, Pallas kernels for 0%

profile of v1, /device:TPU:4, one launch (start us, length us, event | category | flops | bytes accessed | tf_op | source)
XLA Modules:
  0.0 1347.5 jit_solution(6429198725798403510)
XLA Ops:
  7.2 0.0 all-gather.5.cloned.1.call-start
  7.2 1.7 convolution_convert_fusion.1
  8.9 0.0 all-gather.3.cloned.1.call-start
  9.0 0.7 all-gather.3.cloned.1.call-update
  9.7 0.0 reduce-scatter.9.cloned.1.call-start
  10.4 0.8 fusion.63
  11.2 0.8 slice_bitcast_fusion.1
  11.9 156.7 %all-gather.5.cloned.1.call-done = bf16[4096,128]{1,0:T(8,128)(2,1)} async-done(((bf16[128,128]{1,0:T(8,128)(2,1)}), bf16[4096,128]{1,0:T(8,128)(2,1)}) %all-gather.5.cloned.1.call-update) | async-done | bytes 1048592 | tf_op jit(solution)/shard_map/all_gather | solution.py:61
  168.6 3.9 gather_fusion.2
  172.6 5.9 fusion.10
  178.5 4.9 copy.18
  183.4 2.4 fusion.25
  185.8 1.0 copy.14
  186.8 0.0 reduce-scatter.5.cloned.1.call-start
  186.9 137.4 %all-gather.3.cloned.1.call-done = bf16[1,4096,128]{2,1,0:T(8,128)(2,1)} async-done(((bf16[1,128,128]{2,1,0:T(8,128)(2,1)}), bf16[1,4096,128]{2,1,0:T(8,128)(2,1)}) %all-gather.3.cloned.1.call-update) | async-done | bytes 1048592 | tf_op jit(solution)/shard_map/all_gather | solution.py:60
  324.3 3.9 gather_fusion
  328.2 5.9 fusion.14
  334.1 4.9 copy.16
  339.0 2.4 fusion.22
  341.4 0.9 copy.12
  342.4 0.0 reduce-scatter.7.cloned.1.call-start
  342.5 69.6 %reduce-scatter.9.cloned.1.call-done = bf16[128,128]{1,0:T(8,128)(2,1)} async-done(((bf16[2048,128]{1,0:T(8,128)(2,1)}), bf16[128,128]{1,0:T(8,128)(2,1)}) %reduce-scatter.9.cloned.1.call-update) | async-done | bytes 32784 | tf_op jit(solution)/shard_map/reduce_scatter | solution.py:68
  412.1 86.5 %reduce-scatter.5.cloned.1.call-done = bf16[128,128]{1,0:T(8,128)(2,1)} async-done(((bf16[2048,128]{1,0:T(8,128)(2,1)}), bf16[128,128]{1,0:T(8,128)(2,1)}) %reduce-scatter.5.cloned.1.call-update) | async-done | bytes 32784 | tf_op jit(solution)/shard_map/reduce_scatter | solution.py:65
  498.6 0.9 multiply_convert_fusion
  499.5 24.0 %all_gather.13 = bf16[2048,128]{1,0:T(8,128)(2,1)} all-gather(bf16[128,128]{1,0:T(8,128)(2,1)S(1)} %get-tuple-element.9), channel_id=1, replica_groups=mesh['row'=32,'col'=16] {'col'}, dimensions={0}, use_global_device_ids=true | all-gather | bytes 557056 | tf_op jit(solution)/shard_map/all_gather | solution.py:75
  523.6 3.7 gather_fusion.1
  527.3 4.8 fusion.12
  532.1 4.9 copy.17
  537.0 2.4 fusion.16
  539.4 1.4 copy.13
  540.9 0.0 all-reduce.7.cloned.1.call-start
  540.9 0.1 convolution_convert_fusion
  541.1 31.4 %all_gather.15 = bf16[2048,128]{1,0:T(8,128)(2,1)} all-gather(bf16[128,128]{1,0:T(8,128)(2,1)S(1)} %convolution_convert_fusion), channel_id=1, replica_groups=mesh['row'=32,'col'=16] {'col'}, dimensions={0}, use_global_device_ids=true | all-gather | bytes 557056 | tf_op jit(solution)/shard_map/all_gather | solution.py:83
  572.5 3.8 gather_fusion.3
  576.2 0.8 fusion.72
  577.0 132.8 %reduce-scatter.7.cloned.1.call-done = bf16[128,128]{1,0:T(8,128)(2,1)} async-done(((bf16[4096,128]{1,0:T(8,128)(2,1)}), bf16[128,128]{1,0:T(8,128)(2,1)}) %reduce-scatter.7.cloned.1.call-update) | async-done | bytes 32784 | tf_op jit(solution)/shard_map/reduce_scatter | solution.py:77
  709.8 1.6 fusion.29
  711.4 0.2 all-reduce.5.cloned.1.call-start
  711.7 4.8 fusion.8
  716.4 4.9 copy.19
  721.4 159.5 %all-reduce.7.cloned.1.call-done = (f32[128,128]{1,0:T(8,128)}, f32[128,128]{1,0:T(8,128)}) async-done(((f32[128,128]{1,0:T(8,128)}, f32[128,128]{1,0:T(8,128)}), (f32[128,128]{1,0:T(8,128)}, f32[128,128]{1,0:T(8,128)})) %all-reduce.7.cloned.1.call-update) | async-done | bytes 131088 | tf_op jit(solution)/shard_map/psum | solution.py:8
  880.9 0.0 reduce-scatter.11.cloned.1.call-start
  880.9 2.4 fusion.19
  883.4 1.4 copy.15
  884.8 0.8 fusion.28
  885.6 290.9 %all-reduce.5.cloned.1.call-done = (f32[128,128]{1,0:T(8,128)}, f32[128,128]{1,0:T(8,128)}) async-done(((f32[128,128]{1,0:T(8,128)}, f32[128,128]{1,0:T(8,128)}), (f32[128,128]{1,0:T(8,128)}, f32[128,128]{1,0:T(8,128)})) %all-reduce.5.cloned.1.call-update) | async-done | bytes 131088 | tf_op jit(solution)/shard_map/psum | solution.py:7
  1176.5 1.5 broadcast_multiply_fusion
  1178.0 162.7 %reduce-scatter.11.cloned.1.call-done = bf16[128,128]{1,0:T(8,128)(2,1)} async-done(((bf16[4096,128]{1,0:T(8,128)(2,1)}), bf16[128,128]{1,0:T(8,128)(2,1)}) %reduce-scatter.11.cloned.1.call-update) | async-done | bytes 32784 | tf_op jit(solution)/shard_map/reduce_scatter | solution.py:87
  (22 shorter events, 0.2 us)
Async XLA Ops:
  7.2 165.4 %copy-start = (bf16[1,1,96,128,128]{4,3,2,1,0:T(8,128)(2,1)S(1)}, bf16[1,1,96,128,128]{4,3,2,1,0:T(8,128)(2,1)}, u32[]{:S(2)}) copy-start(bf16[1,1,96,128,128]{4,3,2,1,0:T(8,128)(2,1)} %param.10) | copy-start | bytes 9437188
  7.2 161.4 %all-gather.5.cloned.1.call-start = ((), (), s32[]{:S(2)}) async-start(), calls=%async_computation.7 | async-start | bytes 1081344 | tf_op jit(solution)/shard_map/all_gather | solution.py:61
  8.9 315.3 %all-gather.3.cloned.1.call-start = ((), (), s32[]{:S(2)}) async-start(), calls=%async_computation.4 | async-start | bytes 1081344 | tf_op jit(solution)/shard_map/all_gather | solution.py:60
  9.7 402.4 %reduce-scatter.9.cloned.1.call-start = ((), (), s32[]{:S(2)}) async-start(), calls=%async_computation.8 | async-start | bytes 557056 | tf_op jit(solution)/shard_map/reduce_scatter | solution.py:68
  186.8 311.8 %reduce-scatter.5.cloned.1.call-start = ((), (), s32[]{:S(2)}) async-start(), calls=%async_computation.5 | async-start | bytes 557056 | tf_op jit(solution)/shard_map/reduce_scatter | solution.py:65
  339.0 159.5 %copy-start.4 = (bf16[128,128]{1,0:T(8,128)(2,1)S(1)}, bf16[128,128]{1,0:T(8,128)(2,1)}, u32[]{:S(2)}) copy-start(bf16[128,128]{1,0:T(8,128)(2,1)} %param.8) | copy-start | bytes 98308
  342.4 367.4 %reduce-scatter.7.cloned.1.call-start = ((), (), s32[]{:S(2)}) async-start(), calls=%async_computation.6 | async-start | bytes 1081344 | tf_op jit(solution)/shard_map/reduce_scatter | solution.py:77
  540.9 340.0 %all-reduce.7.cloned.1.call-start = ((), (), s32[]{:S(2)}) async-start(), calls=%async_computation.11 | async-start | bytes 262144 | tf_op jit(solution)/shard_map/psum | solution.py:8
  572.5 3.8 copy-start.5
  572.5 137.4 %copy-start.2 = (bf16[1,128,128]{2,1,0:T(8,128)(2,1)S(1)}, bf16[1,128,128]{2,1,0:T(8,128)(2,1)}, u32[]{:S(2)}) copy-start(bf16[1,128,128]{2,1,0:T(8,128)(2,1)} %param.13) | copy-start | bytes 98308
  711.4 465.1 %all-reduce.5.cloned.1.call-start = ((), (), s32[]{:S(2)}) async-start(), calls=%async_computation.10 | async-start | bytes 262144 | tf_op jit(solution)/shard_map/psum | solution.py:7
  880.9 3.9 copy-start.1
  880.9 3.9 copy-start.3
  880.9 459.8 %reduce-scatter.11.cloned.1.call-start = ((), (), s32[]{:S(2)}) async-start(), calls=%async_computation.9 | async-start | bytes 1081344 | tf_op jit(solution)/shard_map/reduce_scatter | solution.py:87
Sparse Core Ops, SparseCore 0:
  10.7 157.9 all-gather.4
  170.7 153.4 all-gather.2
  328.9 83.1 reduce-scatter.8
  417.2 81.2 reduce-scatter.4
  541.0 168.7 reduce-scatter.6
  713.5 167.3 all-reduce.6
  883.8 292.6 all-reduce.4
  1180.1 160.5 reduce-scatter.10
